TPU v7x, 32 devices: a whole 2x2x4 slice. The times are simulated.
32 devices in a mesh: dp: 16 (over z, x, core), head: 2 (over y).
Axes of the slice: x: 2, y: 2, z: 4, core: 2. Of those that a mesh axis runs over, the one named last changes fastest.
Arguments:
- tokens: bfloat16 [16384, 1024], P(('dp', 'head')), may hold values from -6 to 6
- lengths: int32 [16], P('dp'), may hold values from 128 to 1024, as said below
- decay: float32 [8], P('head'), may hold values from 0.00048828125 to 0.03125
- w_query: bfloat16 [1024, 1024], P(None, 'head'), may hold values from -0.1875 to 0.1875
- w_key: bfloat16 [1024, 1024], P(None, 'head'), may hold values from -0.1875 to 0.1875
- w_value: bfloat16 [1024, 1024], P(None, 'head'), may hold values from -0.1875 to 0.1875
- w_gate: bfloat16 [1024, 1024], P(None, 'head'), may hold values from -0.1875 to 0.1875
- w_out: bfloat16 [1024, 1024], P('head'), may hold values from -0.1875 to 0.1875
- f_value: bfloat16 [1024, 2816], P('dp', 'head'), may hold values from -0.1875 to 0.1875
- f_gate: bfloat16 [1024, 2816], P('dp', 'head'), may hold values from -0.1875 to 0.1875
- f_out: bfloat16 [2816, 1024], P('head', 'dp'), may hold values from -0.109375 to 0.109375
- cotangent: bfloat16 [16384, 1024], P(('dp', 'head')), may hold values from -6 to 6
Outputs:
- output: bfloat16 [16384, 1024], P(('dp', 'head'))
- d_tokens: float32 [16384, 1024], P(('dp', 'head'))
- d_w_query: float32 [1024, 1024], P(None, 'head')
- d_w_key: float32 [1024, 1024], P(None, 'head')
- d_w_value: float32 [1024, 1024], P(None, 'head')
- d_w_gate: float32 [1024, 1024], P(None, 'head')
- d_w_out: float32 [1024, 1024], P('head')
- d_f_value: float32 [1024, 2816], P('dp', 'head')
- d_f_gate: float32 [1024, 2816], P('dp', 'head')
- d_f_out: float32 [2816, 1024], P('head', 'dp')
Inputs may be any that keep to these rules, and one draw needn't show every extreme that they name: `lengths`: each bucket holds a single slot, and that slot's sequence has length 1024.
All inputs are finite; a program needn't handle non-finite values.
Results may differ from a plain program's by a relative error of at most 0.022.
Values may be sent and summed in bfloat16 or wider, within the bound.
A program may use at most 192 MiB of HBM per device.

v0:
```python
import jax
import jax.numpy as jnp
from jax import lax
from jax.sharding import PartitionSpec as P

D = 1024
HD = 128
SEQ_DEV = 1
SLOT = 1024
BLOCK = 512
epsilon = 1e-06


def normalize(values):
    factor = lax.rsqrt(jnp.mean(values * values, axis=-1, keepdims=True) + epsilon)
    return (values * factor, factor)


def norm_back(grad_normed, normed, factor):
    inner_sum = jnp.mean(grad_normed * normed, axis=-1, keepdims=True)
    return factor * (grad_normed - normed * inner_sum)


def silu_slope(values):
    sigmoid = jax.nn.sigmoid(values)
    return sigmoid * (1.0 + values * (1.0 - sigmoid))


def matmul(left_side, right_side):
    return jnp.dot(left_side, right_side, preferred_element_type=jnp.float32)


def matmul_right_t(left_side, right_side):
    return lax.dot_general(
        left_side, right_side, (((1,), (1,)), ((), ())), preferred_element_type=jnp.float32
    )


def matmul_left_t(left_side, right_side):
    return lax.dot_general(
        left_side, right_side, (((0,), (0,)), ((), ())), preferred_element_type=jnp.float32
    )


def exact(form, left_side, right_side):
    return jnp.einsum(form, left_side, right_side, precision=lax.Precision.HIGHEST)


def decay_tables(rates):
    offsets = jnp.arange(BLOCK).astype(jnp.float32)
    spread = offsets[:, None] - offsets[None, :]
    causal = spread >= 0
    within = jnp.where(
        causal[None], jnp.exp(-rates[:, None, None] * jnp.where(causal, spread, 0.0)[None]), 0.0
    )
    first_decay = jnp.exp(-rates[:, None] * (offsets[None, :] + 1.0))
    last_decay = jnp.exp(-rates[:, None] * (BLOCK - 1.0 - offsets[None, :]))
    block_decay = jnp.exp(-rates * BLOCK)
    return (within, first_decay, last_decay, block_decay)


def to_blocks(values, heads):
    shaped = values.reshape(SEQ_DEV, SLOT // BLOCK, BLOCK, heads, HD)
    return shaped.transpose(1, 0, 3, 2, 4)


def from_blocks(blocks):
    return blocks.transpose(1, 0, 3, 2, 4).reshape(-1, blocks.shape[2] * blocks.shape[4])


def lightning_forward(query, keys, values, tables):
    within, first_decay, last_decay, block_decay = tables

    def advance(carried, inputs):
        query_blk, keys_blk, values_blk = inputs
        scores = jnp.einsum(
            "shbd,shcd->shbc", query_blk, keys_blk, preferred_element_type=jnp.float32
        )
        weights = (scores * within[None]).astype(jnp.bfloat16)
        inner_sum = jnp.einsum(
            "shbc,shcd->shbd", weights, values_blk, preferred_element_type=jnp.float32
        )
        outer_sum = first_decay[None, :, :, None] * exact(
            "shbd,shde->shbe", query_blk.astype(jnp.float32), carried
        )
        keys_scaled = keys_blk.astype(jnp.float32) * last_decay[None, :, :, None]
        update = exact("shbd,shbe->shde", keys_scaled, values_blk.astype(jnp.float32))
        return (
            block_decay[None, :, None, None] * carried + update,
            (inner_sum + outer_sum, carried),
        )

    initial = jnp.zeros((SEQ_DEV, query.shape[2], HD, HD), jnp.float32)
    final_state, (mixed, states) = lax.scan(advance, initial, (query, keys, values))
    return (mixed, states)


def lightning_backward(query, keys, values, grads, states, tables):
    within, first_decay, last_decay, block_decay = tables

    def retreat(later_grad, inputs):
        query_blk, keys_blk, values_blk, grad_blk, carried = inputs
        scores = jnp.einsum(
            "shbd,shcd->shbc", query_blk, keys_blk, preferred_element_type=jnp.float32
        )
        weights = (scores * within[None]).astype(jnp.bfloat16)
        d_weights = jnp.einsum(
            "shbd,shcd->shbc", grad_blk, values_blk, preferred_element_type=jnp.float32
        )
        d_scores = (d_weights * within[None]).astype(jnp.bfloat16)
        d_query = jnp.einsum(
            "shbc,shcd->shbd", d_scores, keys_blk, preferred_element_type=jnp.float32
        )
        d_keys = jnp.einsum(
            "shbc,shbd->shcd", d_scores, query_blk, preferred_element_type=jnp.float32
        )
        d_values = jnp.einsum(
            "shbc,shbd->shcd", weights, grad_blk, preferred_element_type=jnp.float32
        )
        grad_scaled = grad_blk.astype(jnp.float32) * first_decay[None, :, :, None]
        keys_scaled = keys_blk.astype(jnp.float32) * last_decay[None, :, :, None]
        d_query = d_query + exact("shbe,shde->shbd", grad_scaled, carried)
        d_keys = d_keys + last_decay[None, :, :, None] * exact(
            "shbe,shde->shbd", values_blk.astype(jnp.float32), later_grad
        )
        d_values = d_values + exact("shbd,shde->shbe", keys_scaled, later_grad)
        earlier = block_decay[None, :, None, None] * later_grad + exact(
            "shbd,shbe->shde", query_blk.astype(jnp.float32), grad_scaled
        )
        return (earlier, (d_query, d_keys, d_values))

    initial = jnp.zeros((SEQ_DEV, query.shape[2], HD, HD), jnp.float32)
    first_grad, results = lax.scan(
        retreat, initial, (query, keys, values, grads, states), reverse=True
    )
    return results


def body(
    tokens,
    lengths,
    decay,
    w_query,
    w_key,
    w_value,
    w_gate,
    w_out,
    f_value,
    f_gate,
    f_out,
    cotangent,
):
    own_rows = tokens.shape[0]
    first_row = lax.axis_index("head") * own_rows
    heads_here = decay.shape[0]
    tables = decay_tables(decay)
    positions = first_row + jnp.arange(own_rows, dtype=jnp.int32)
    slot_match = (positions // SLOT)[:, None] == jnp.arange(SEQ_DEV, dtype=jnp.int32)[None, :]
    length_of = jnp.sum(jnp.where(slot_match, lengths[None, :], 0), axis=1)
    keep_rows = (positions % SLOT < length_of).astype(jnp.float32)[:, None]
    inputs_f = tokens.astype(jnp.float32)
    normed, scale_in = normalize(inputs_f)
    gathered = lax.all_gather(normed.astype(jnp.bfloat16), "head", axis=0, tiled=True)
    query_pre = matmul(gathered, w_query)
    keys_pre = matmul(gathered, w_key)
    values_pre = matmul(gathered, w_value)
    gate_pre = matmul(gathered, w_gate)
    query_blocks = to_blocks(jax.nn.silu(query_pre).astype(jnp.bfloat16), heads_here)
    keys_blocks = to_blocks(jax.nn.silu(keys_pre).astype(jnp.bfloat16), heads_here)
    values_blocks = to_blocks(values_pre.astype(jnp.bfloat16), heads_here)
    mixed_blocks, states = lightning_forward(query_blocks, keys_blocks, values_blocks, tables)
    mixed = from_blocks(mixed_blocks)
    squares = lax.psum(jnp.sum(mixed * mixed, axis=1), "head")
    scale_out = lax.rsqrt(squares / D + epsilon)[:, None]
    mixed_unit = mixed * scale_out
    gated = (mixed_unit * gate_pre).astype(jnp.bfloat16)
    branch = lax.psum_scatter(
        matmul(gated, w_out).astype(jnp.bfloat16), "head", scatter_dimension=0, tiled=True
    ).astype(jnp.float32)
    middle = inputs_f + branch
    mid_normed, scale_mid = normalize(middle)
    mid_all = lax.all_gather(mid_normed.astype(jnp.bfloat16), "head", axis=0, tiled=True)
    value_full, gate_full = (
        lax.all_gather(f_value, "dp", axis=0, tiled=True),
        lax.all_gather(f_gate, "dp", axis=0, tiled=True),
    )
    down_full = lax.all_gather(f_out, "dp", axis=1, tiled=True)
    value_ffn = matmul(mid_all, value_full)
    gate_ffn = matmul(mid_all, gate_full)
    hidden = (value_ffn * gate_ffn).astype(jnp.bfloat16)
    ffn_branch = lax.psum_scatter(
        matmul(hidden, down_full).astype(jnp.bfloat16), "head", scatter_dimension=0, tiled=True
    ).astype(jnp.float32)
    output = ((middle + ffn_branch) * keep_rows).astype(jnp.bfloat16)
    grad_out = cotangent.astype(jnp.float32) * keep_rows
    grad_all = lax.all_gather(grad_out.astype(jnp.bfloat16), "head", axis=0, tiled=True)
    grad_hidden = matmul_right_t(grad_all, down_full)
    d_value_ffn = (grad_hidden * gate_ffn).astype(jnp.bfloat16)
    d_gate_ffn = (grad_hidden * value_ffn).astype(jnp.bfloat16)
    d_mid_normed = lax.psum_scatter(
        (matmul_right_t(d_value_ffn, value_full) + matmul_right_t(d_gate_ffn, gate_full)).astype(
            jnp.bfloat16
        ),
        "head",
        scatter_dimension=0,
        tiled=True,
    ).astype(jnp.float32)
    grad_middle = grad_out + norm_back(d_mid_normed, mid_normed, scale_mid)
    joined = jnp.concatenate([d_value_ffn, d_gate_ffn], axis=1)
    hidden_here = hidden.shape[1]
    shares = lax.psum_scatter(
        jnp.concatenate(
            [matmul_left_t(mid_all, joined), matmul_left_t(grad_all, hidden)], axis=1
        ).astype(jnp.bfloat16),
        "dp",
        scatter_dimension=0,
        tiled=True,
    ).astype(jnp.float32)
    d_f_value = shares[:, :hidden_here]
    d_f_gate = shares[:, hidden_here : 2 * hidden_here]
    d_f_out = shares[:, 2 * hidden_here :].T
    grad_rows = lax.all_gather(grad_middle.astype(jnp.bfloat16), "head", axis=0, tiled=True)
    d_gated = matmul_right_t(grad_rows, w_out)
    d_w_out_local = matmul_left_t(gated, grad_rows)
    d_gate_pre = (d_gated * mixed_unit).astype(jnp.bfloat16)
    d_unit = d_gated * gate_pre
    inner_out = lax.psum(jnp.sum(d_unit * mixed_unit, axis=1), "head")
    d_mixed = (scale_out * (d_unit - mixed_unit * (inner_out / D)[:, None])).astype(jnp.bfloat16)
    d_query, d_keys, d_values = lightning_backward(
        query_blocks, keys_blocks, values_blocks, to_blocks(d_mixed, heads_here), states, tables
    )
    d_query_pre = (from_blocks(d_query) * silu_slope(query_pre)).astype(jnp.bfloat16)
    d_keys_pre = (from_blocks(d_keys) * silu_slope(keys_pre)).astype(jnp.bfloat16)
    d_values_pre = from_blocks(d_values).astype(jnp.bfloat16)
    total = matmul_right_t(d_query_pre, w_query) + matmul_right_t(d_keys_pre, w_key)
    d_normed = lax.psum_scatter(
        (total + matmul_right_t(d_values_pre, w_value) + matmul_right_t(d_gate_pre, w_gate)).astype(
            jnp.bfloat16
        ),
        "head",
        scatter_dimension=0,
        tiled=True,
    ).astype(jnp.float32)
    d_tokens = grad_middle + norm_back(d_normed, normed, scale_in)
    grads_attention = (
        lax.psum(matmul_left_t(gathered, d_query_pre).astype(jnp.bfloat16), "dp").astype(
            jnp.float32
        ),
        lax.psum(matmul_left_t(gathered, d_keys_pre).astype(jnp.bfloat16), "dp").astype(
            jnp.float32
        ),
        lax.psum(matmul_left_t(gathered, d_values_pre).astype(jnp.bfloat16), "dp").astype(
            jnp.float32
        ),
        lax.psum(matmul_left_t(gathered, d_gate_pre).astype(jnp.bfloat16), "dp").astype(
            jnp.float32
        ),
        lax.psum(d_w_out_local.astype(jnp.bfloat16), "dp").astype(jnp.float32),
    )
    return (
        output,
        d_tokens,
        grads_attention[0],
        grads_attention[1],
        grads_attention[2],
        grads_attention[3],
        grads_attention[4],
        d_f_value,
        d_f_gate,
        d_f_out,
    )


def solution(mesh):
    placed = (
        P(("dp", "head"), None),
        P("dp"),
        P("head"),
        P(None, "head"),
        P(None, "head"),
        P(None, "head"),
        P(None, "head"),
        P("head", None),
        P("dp", "head"),
        P("dp", "head"),
        P("head", "dp"),
        P(("dp", "head"), None),
    )
    return jax.shard_map(
        body,
        mesh=mesh,
        in_specs=placed,
        out_specs=(
            P(("dp", "head"), None),
            P(("dp", "head"), None),
            P(None, "head"),
            P(None, "head"),
            P(None, "head"),
            P(None, "head"),
            P("head", None),
            P("dp", "head"),
            P("dp", "head"),
            P("head", "dp"),
        ),
        check_vma=False,
    )
```

profile of v0, /device:TPU:0, one launch (start us, length us, event | category | flops | bytes accessed | tf_op | source)
XLA Modules:
  0.0 686.0 jit_solution(16797415050043910649)
XLA Ops:
  15.0 33.8 %all-gather.8.cloned.1.call-done = bf16[1024,1024]{1,0:T(8,128)(2,1)} async-done(((bf16[512,1024]{1,0:T(8,128)(2,1)}), bf16[1024,1024]{1,0:T(8,128)(2,1)}) %all-gather.8.cloned.1.call-update) | async-done | bytes 2097168 | tf_op jit(solution)/shard_map/all_gather | solution.py:163
  48.8 4.4 multiply_convert_fusion.8
  53.4 3.1 convolution_convert_fusion.8
  59.1 2.8 copy_bitcast_fusion.1
  61.9 3.1 multiply_convert_fusion.7
  69.1 15.1 %while.40 = (s32[]{:T(128)}, f32[1,4,128,128]{3,2,1,0:T(8,128)S(1)}, f32[2,1,4,512,128]{4,3,2,1,0:T(8,128)}, f32[2,1,4,128,128]{4,3,2,1,0:T(8,128)}, f32[4]{0:T(...) while((s32[]{:T(128)}, ...), condition=%wide.region_2.3_spmd.clone.clone.clone, body=%wide.region_1.2_spmd.clone.clone.clone.sunk | while | flops 1347751936 | bytes 17343232 | solution.py:94
  69.1 3.0 fusion.246
  72.2 2.7 fusion.247
  76.6 3.0 fusion.246
  79.8 2.7 fusion.247
  86.4 4.1 copy.42
  92.6 5.1 psum.49
  97.7 4.5 multiply_convert_fusion.6
  106.5 31.3 %reduce-scatter.6.cloned.1.call-done = bf16[512,1024]{1,0:T(8,128)(2,1)} async-done(((bf16[1024,1024]{1,0:T(8,128)(2,1)}), bf16[512,1024]{1,0:T(8,128)(2,1)}) %reduce-scatter.6.cloned.1.call-update) | async-done | bytes 1048592 | tf_op jit(solution)/shard_map/reduce_scatter | solution.py:177
  145.4 7.4 %all-gather.12.cloned.1.call-done = bf16[1024,1408]{1,0:T(8,128)(2,1)} async-done(((bf16[64,1408]{1,0:T(8,128)(2,1)}), bf16[1024,1408]{1,0:T(8,128)(2,1)}) %all-gather.12.cloned.1.call-update) | async-done | bytes 2883600 | tf_op jit(solution)/shard_map/all_gather | solution.py:184
  152.9 33.7 %all-gather.10.cloned.1.call-done = bf16[1024,1024]{1,0:T(8,128)(2,1)} async-done(((bf16[512,1024]{1,0:T(8,128)(2,1)}), bf16[1024,1024]{1,0:T(8,128)(2,1)}) %all-gather.10.cloned.1.call-update) | async-done | bytes 2097168 | tf_op jit(solution)/shard_map/all_gather | solution.py:182
  186.6 8.3 %fusion.155 = f32[1024,1408]{1,0:T(8,128)} fusion(bf16[1024,1024]{1,0:T(8,128)(2,1)} %all-gather.10.cloned.1.call-done, bf16[1024,1408]{1,0:T(8,128)(2,1)} %all-gather.12.cloned.1.call-done), kind=kOutput, calls=%fused_computation.209 | convolution fusion | flops 2952790016 | bytes 10747904 | tf_op jit(solution)/shard_map/dot_general | solution.py:30
  194.9 38.1 %all-gather.14.cloned.1.call-done = bf16[1024,1408]{1,0:T(8,128)(2,1)} async-done(((bf16[64,1408]{1,0:T(8,128)(2,1)}), bf16[1024,1408]{1,0:T(8,128)(2,1)}) %all-gather.14.cloned.1.call-update) | async-done | bytes 2883600 | tf_op jit(solution)/shard_map/all_gather | solution.py:185
  233.0 8.4 %fusion.156 = f32[1024,1408]{1,0:T(8,128)} fusion(bf16[1024,1024]{1,0:T(8,128)(2,1)} %all-gather.10.cloned.1.call-done, bf16[1024,1408]{1,0:T(8,128)(2,1)} %all-gather.14.cloned.1.call-done), kind=kOutput, calls=%fused_computation.210 | convolution fusion | flops 2952790016 | bytes 10747904 | tf_op jit(solution)/shard_map/dot_general | solution.py:30
  241.4 25.5 %all-gather.18.cloned.1.call-done = bf16[1024,1024]{1,0:T(8,128)(2,1)} async-done(((bf16[512,1024]{1,0:T(8,128)(2,1)}), bf16[1024,1024]{1,0:T(8,128)(2,1)}) %all-gather.18.cloned.1.call-update) | async-done | bytes 2097168 | tf_op jit(solution)/shard_map/all_gather | solution.py:196
  266.8 46.6 %all-gather.16.cloned.1.call-done = bf16[1408,1024]{0,1:T(8,128)(2,1)} async-done(((bf16[1408,64]{0,1:T(8,128)(2,1)}), bf16[1408,1024]{0,1:T(8,128)(2,1)}) %all-gather.16.cloned.1.call-update) | async-done | bytes 2883600 | tf_op jit(solution)/shard_map/all_gather | solution.py:187
  313.4 11.0 %multiply_convert_fusion = (bf16[1024,1408]{1,0:T(8,128)(2,1)S(1)}, bf16[1024,1408]{1,0:T(8,128)(2,1)}, bf16[1024,1408]{1,0:T(8,128)(2,1)S(1)}) fusion(f32[1024,1408]{1,0:T(8,128)} %fusion.155, f32[1024,1408]{1,0:T(8,128)} %fusion.156, bf16[1024,1024]{1,0:T(8,128)(2,1)} %all-gather.18.cloned.1.call-done, bf16[1408,1024]{0,1:T(8,128)(2,1)} %all-gather.16.cloned.1.call-done), kind=kOutput, calls=%fused_computation.120 | convolution fusion | flops 2961440768 | bytes 25165824 | tf_op jit(solution)/shard_map/dot_general | solution.py:34
  324.4 3.4 fusion.157
  328.3 4.6 add_convert_fusion.1
  333.0 30.6 %reduce-scatter.10.cloned.1.call-done = bf16[512,1024]{1,0:T(8,128)(2,1)} async-done(((bf16[1024,1024]{1,0:T(8,128)(2,1)}), bf16[512,1024]{1,0:T(8,128)(2,1)}) %reduce-scatter.10.cloned.1.call-update) | async-done | bytes 1048592 | tf_op jit(solution)/shard_map/reduce_scatter | solution.py:200
  371.5 29.3 %all-gather.20.cloned.1.call-done = bf16[1024,1024]{1,0:T(8,128)(2,1)} async-done(((bf16[512,1024]{1,0:T(8,128)(2,1)}), bf16[1024,1024]{1,0:T(8,128)(2,1)}) %all-gather.20.cloned.1.call-update) | async-done | bytes 2097168 | tf_op jit(solution)/shard_map/all_gather | solution.py:222
  400.8 5.3 multiply_reduce_fusion
  406.1 4.9 psum.50
  418.9 36.7 %while.41 = (s32[]{:T(128)}, f32[1,4,128,128]{3,2,1,0:T(8,128)S(1)}, f32[2,1,4,512,128]{4,3,2,1,0:T(8,128)}, f32[2,1,4,512,128]{4,3,2,1,0:T(8,128)}, bf16[2,1,4,...) while((s32[]{:T(128)}, ...), condition=%wide.region_13.14_spmd.clone.clone.clone, body=%wide.region_12.13_spmd.clone.clone.clone.sunk | while | flops 2964131840 | bytes 44889964 | solution.py:133
  418.9 2.8 fusion.264
  422.8 2.7 fusion.268
  426.5 3.3 fusion.266
  429.9 3.3 fusion.269
  437.2 2.8 fusion.264
  441.0 2.7 fusion.268
  444.8 3.3 fusion.266
  448.1 3.3 fusion.269
  455.6 2.9 copy.45
  458.6 3.0 copy.44
  483.7 2.7 add_convert_fusion
  486.5 7.5 %convolution_convert_fusion.1 = bf16[1024,1024]{1,0:T(8,128)(2,1)} fusion(bf16[1024,1408]{1,0:T(8,128)(2,1)} %get-tuple-element.714, bf16[1408,1024]{0,1:T(8,128)(2,1)} %all-gather.16.cloned.1.call-done), kind=kOutput, calls=%fused_computation.160 | convolution fusion | flops 2953838592 | bytes 7864320 | tf_op jit(solution)/shard_map/dot_general | solution.py:30
  495.7 5.7 convolution_convert_fusion
  501.4 6.8 fusion.121
  508.3 3.8 pad_maximum_fusion
  512.1 115.8 %all-reduce.3.cloned.1.call-done = (bf16[1024,512]{1,0:T(8,128)(2,1)}, bf16[1024,512]{1,0:T(8,128)(2,1)}, bf16[1024,512]{1,0:T(8,128)(2,1)}, bf16[1024,512]{1,0:T(8,128)(2,1)}, bf16[512,1024]{1,0:T(8,128)(2,1)}) async-done(((bf16[1024,512]{1,0:T(8,128)(2,1)}, bf16[1024,512]{1,0:T(8,128)(2,1)}, bf16[1024,512]{1,0:T(8,128)(2,1)}, bf16[1024,512]{1,0:T(8,128)(2,1)}, bf16[512,1024]{1,0:T(8,128)(2,1)}), ...) | async-done | bytes 5242896 | tf_op jit(solution)/shard_map/psum | solution.py:246
  627.8 2.9 convert_element_type.243
  639.0 4.5 fusion.131
  643.4 31.9 %reduce-scatter.14.cloned.1.call-done = bf16[64,4224]{1,0:T(8,128)(2,1)} async-done(((bf16[1024,4224]{1,0:T(8,128)(2,1)}), bf16[64,4224]{1,0:T(8,128)(2,1)}) %reduce-scatter.14.cloned.1.call-update) | async-done | bytes 540688 | tf_op jit(solution)/shard_map/reduce_scatter | solution.py:211
  (222 shorter events, 95.5 us)
Async XLA Ops:
  8.0 95.2 %copy-start = (bf16[512,1024]{1,0:T(8,128)(2,1)S(1)}, bf16[512,1024]{1,0:T(8,128)(2,1)}, u32[]{:S(2)}) copy-start(bf16[512,1024]{1,0:T(8,128)(2,1)} %param.23) | copy-start | bytes 3145732
  8.0 40.8 %all-gather.8.cloned.1.call-start = ((), (), s32[]{:S(2)}) async-start(), calls=%async_computation.5 | async-start | bytes 3145728 | tf_op jit(solution)/shard_map/all_gather | solution.py:163
  8.1 4.8 copy-start.51
  10.3 38.5 %copy-start.48 = (bf16[1024,512]{1,0:T(8,128)(2,1)S(1)}, bf16[1024,512]{1,0:T(8,128)(2,1)}, u32[]{:S(2)}) copy-start(bf16[1024,512]{1,0:T(8,128)(2,1)} %param.20) | copy-start | bytes 3145732
  12.8 125.0 %reduce-scatter.6.cloned.1.call-start = ((), (), s32[]{:S(2)}) async-start(), calls=%async_computation.6 | async-start | bytes 3145728 | tf_op jit(solution)/shard_map/reduce_scatter | solution.py:177
  59.1 2.8 copy-start.32
  59.1 2.8 copy-start.47
  66.3 2.7 copy-start.16
  72.1 2.9 copy-start.21
  72.1 3.7 copy-start.13
  79.7 2.8 copy-start.21
  79.7 3.7 copy-start.13
  84.2 6.3 copy-start.6
  92.5 9.6 %copy-start.4 = (f32[64,8,2,512]{3,1,2,0:T(8,128)}, f32[64,8,2,512]{3,1,2,0:T(8,128)S(1)}, u32[]{:S(2)}) copy-start(f32[64,8,2,512]{3,1,2,0:T(8,128)S(1)} %copy.52) | copy-start | bytes 6291460
  105.8 32.0 %copy-start.2 = (bf16[512,1024]{1,0:T(8,128)(2,1)S(1)}, bf16[512,1024]{1,0:T(8,128)(2,1)}, u32[]{:S(2)}) copy-start(bf16[512,1024]{1,0:T(8,128)(2,1)} %param.16) | copy-start | bytes 3145732
  105.8 47.0 %all-gather.12.cloned.1.call-start = ((), (), s32[]{:S(2)}) async-start(), calls=%async_computation.8 | async-start | bytes 3063808 | tf_op jit(solution)/shard_map/all_gather | solution.py:184
  106.4 80.2 %all-gather.10.cloned.1.call-start = ((), (), s32[]{:S(2)}) async-start(), calls=%async_computation.7 | async-start | bytes 3145728 | tf_op jit(solution)/shard_map/all_gather | solution.py:182
  140.8 92.1 %all-gather.14.cloned.1.call-start = ((), (), s32[]{:S(2)}) async-start(), calls=%async_computation.9 | async-start | bytes 3063808 | tf_op jit(solution)/shard_map/all_gather | solution.py:185
  141.4 125.4 %all-gather.18.cloned.1.call-start = ((), (), s32[]{:S(2)}) async-start(), calls=%async_computation.12 | async-start | bytes 3145728 | tf_op jit(solution)/shard_map/all_gather | solution.py:196
  144.6 168.8 %all-gather.16.cloned.1.call-start = ((), (), s32[]{:S(2)}) async-start(), calls=%async_computation.10 | async-start | bytes 3063808 | tf_op jit(solution)/shard_map/all_gather | solution.py:187
  145.4 218.3 %reduce-scatter.10.cloned.1.call-start = ((), (), s32[]{:S(2)}) async-start(), calls=%async_computation.13 | async-start | bytes 3145728 | tf_op jit(solution)/shard_map/reduce_scatter | solution.py:200
  313.4 11.0 %copy-start.44 = (bf16[1024,1408]{1,0:T(8,128)(2,1)S(1)}, bf16[1024,1408]{1,0:T(8,128)(2,1)}, u32[]{:S(2)}) copy-start(bf16[1024,1408]{1,0:T(8,128)(2,1)} %all-gather.12.cloned.1.call-done) | copy-start | bytes 8650756
  324.4 3.5 copy-start.27
  324.4 3.5 copy-start.25
  324.4 3.9 copy-start.45
  333.0 67.8 %all-gather.20.cloned.1.call-start = ((), (), s32[]{:S(2)}) async-start(), calls=%async_computation.14 | async-start | bytes 3145728 | tf_op jit(solution)/shard_map/all_gather | solution.py:222
  367.5 33.3 %copy-start.5 = (f32[64,8,2,512]{3,1,2,0:T(8,128)S(1)}, f32[64,8,2,512]{3,1,2,0:T(8,128)}, u32[]{:S(2)}) copy-start(f32[64,8,2,512]{3,1,2,0:T(8,128)} %copy-done.4) | copy-start | bytes 6291460
  367.5 260.3 %all-reduce.3.cloned.1.call-start = ((), (), s32[]{:S(2)}) async-start(), calls=%async_computation.17 | async-start | bytes 10485760 | tf_op jit(solution)/shard_map/psum | solution.py:246
  418.9 2.8 copy-start.7
  422.7 2.8 copy-start.9
  426.2 3.7 copy-start.8
  426.2 3.7 copy-start.10
  437.2 2.8 copy-start.7
  441.0 2.8 copy-start.9
  444.5 3.7 copy-start.8
  444.5 3.7 copy-start.10
  458.5 3.1 copy-start.19
  462.4 11.0 %copy-start.38 = (bf16[1,2,512,4,128]{4,3,2,1,0:T(4,128)(2,1)}, bf16[1,2,512,4,128]{4,3,2,1,0:T(4,128)(2,1)S(1)}, u32[]{:S(2)}) copy-start(bf16[1,2,512,4,128]{4,3,2,1,0:T(4,128)(2,1)S(1)} %copy.46) | copy-start | bytes 3145732
  478.0 159.2 %reduce-scatter.12.cloned.1.call-start = ((), (), s32[]{:S(2)}) async-start(), calls=%async_computation.15 | async-start | bytes 3145728 | tf_op jit(solution)/shard_map/reduce_scatter | solution.py:236
  478.3 2.6 copy-start.49
  486.5 152.5 %reduce-scatter.8.cloned.1.call-start = ((), (), s32[]{:S(2)}) async-start(), calls=%async_computation.11 | async-start | bytes 3145728 | tf_op jit(solution)/shard_map/reduce_scatter | solution.py:191
  494.1 181.3 %reduce-scatter.14.cloned.1.call-start = ((), (), s32[]{:S(2)}) async-start(), calls=%async_computation.16 | async-start | bytes 9191424 | tf_op jit(solution)/shard_map/reduce_scatter | solution.py:211
  495.7 5.7 copy-start.26
  495.7 5.7 copy-start.28
  495.7 5.7 copy-start.46
  627.8 2.9 copy-start.37
  635.6 3.3 copy-start.12
  639.0 39.3 %copy-start.1 = (bf16[512,1024]{1,0:T(8,128)(2,1)S(1)}, bf16[512,1024]{1,0:T(8,128)(2,1)}, u32[]{:S(2)}) copy-start(bf16[512,1024]{1,0:T(8,128)(2,1)} %param.23) | copy-start | bytes 3145732
  (25 other events, 37.9 us)
Sparse Core Ops, SparseCore 0:
  12.9 35.8 all-gather.7
  106.0 31.7 reduce-scatter.5
  333.1 30.4 reduce-scatter.9
  367.6 33.1 all-gather.19
  486.6 31.8 reduce-scatter.11
  520.7 31.8 reduce-scatter.7
  557.2 118.1 reduce-scatter.13
Sparse Core Ops, SparseCore 1:
  108.9 43.9 all-gather.11
  154.9 31.6 all-gather.9
  189.0 43.9 all-gather.13
  235.2 31.6 all-gather.17
  269.4 43.9 all-gather.15
  478.1 149.7 all-reduce.2
where the time goes:
time: 694 us; the launch traced here: 686 us
  waiting for transfers between devices  426 us (61%)
  matrix products  147 us (21%)
  other arithmetic  43.4 us (6%)
  local copies, waits for them, and re-layouts  41 us (6%)
  between operations  17.1 us (2%)
  blocking collectives  10 us (1%)
    psum x1, waiting for transfers between devices, body(): lax.psum(matmul_left_t(gathered, d_query_pre).astype(jnp.bfloat16), 'dp')  116 us
    all_gather x1, waiting for transfers between devices, body(): down_full = lax.all_gather(f_out, 'dp', axis=1, tiled=True)  46.6 us
    dot_general x8, matrix products, matmul(): return jnp.dot(left_side, right_side, preferred_element_type=jnp.float32)  41.9 us
    all_gather x1, waiting for transfers between devices, body(): lax.all_gather(f_gate, 'dp', axis=0, tiled=True)  38.1 us
    all_gather x1, waiting for transfers between devices, body(): lax.all_gather(normed.astype(jnp.bfloat16), 'head', axis=0, tiled=True)  33.8 us
    all_gather x1, waiting for transfers between devices, body(): lax.all_gather(mid_normed.astype(jnp.bfloat16), 'head', axis=0, tiled=True)  33.7 us
    dot_general x8, matrix products, matmul_right_t(): lax.dot_general(left_side, right_side, (((1,), (1,)), ((), ())), preferre...  32.3 us
    reduce_scatter x1, waiting for transfers between devices, body(): lax.psum_scatter(jnp.concatenate([matmul_left_t(mid_all, joined), matmul_...  31.9 us
  transfers between devices with their start and end apart: 13, of which 11 were waited for; matrix products, arithmetic and copies ran while one was open for 11% of the time, Pallas kernels for 0%

commit v1 on v0

--- a/solution.py
+++ b/solution.py
@@ -9,6 +9,19 @@
 SLOT = 1024
 BLOCK = 512
 epsilon = 1e-06
+
+
+def ring_gather(value, axis, dim):
+    ways = lax.axis_size(axis)
+    up = [(d, (d + 1) % ways) for d in range(ways)]
+    down = [(d, (d - 1) % ways) for d in range(ways)]
+    earlier, later = ([value], [value])
+    for _ in range(ways // 2):
+        earlier.append(lax.ppermute(earlier[-1], axis, up))
+    for _ in range((ways - 1) // 2):
+        later.append(lax.ppermute(later[-1], axis, down))
+    line = jnp.concatenate([*earlier[::-1], *later[1:]], axis=dim)
+    return jnp.roll(line, (lax.axis_index(axis) - ways // 2) * value.shape[dim], axis=dim)
 
 
 def normalize(values):
@@ -182,7 +195,7 @@
     mid_all = lax.all_gather(mid_normed.astype(jnp.bfloat16), "head", axis=0, tiled=True)
     value_full, gate_full = (
         lax.all_gather(f_value, "dp", axis=0, tiled=True),
-        lax.all_gather(f_gate, "dp", axis=0, tiled=True),
+        ring_gather(f_gate, "dp", 0),
     )
     down_full = lax.all_gather(f_out, "dp", axis=1, tiled=True)
     value_ffn = matmul(mid_all, value_full)

time: 694 us -> 797 us (1.15)
  waiting for transfers between devices: 426 us -> 469 us
  starting transfers between devices: 1.41 us -> 33 us
  local copies, waits for them, and re-layouts: 41 us -> 71.2 us
    reduce_scatter x1, waiting for transfers between devices: 31.9 us -> 107 us  [body(): lax.psum_scatter(jnp.concatenate([matmul_left_t(mid_all, joined), matmul_...]
    all_gather x1 -> x0, waiting for transfers between devices: 38.1 us -> none  [body(): lax.all_gather(f_gate, 'dp', axis=0, tiled=True)]
    all_gather x1, waiting for transfers between devices: 46.6 us -> 14 us  [body(): down_full = lax.all_gather(f_out, 'dp', axis=1, tiled=True)]
    reduce_scatter x1, waiting for transfers between devices: 0.02 us -> 32.4 us  [body(): lax.psum_scatter(matmul(hidden, down_full).astype(jnp.bfloat16), 'head',...]
    reduce_scatter x1, waiting for transfers between devices: 31.3 us -> 0.01 us  [body(): lax.psum_scatter(matmul(gated, w_out).astype(jnp.bfloat16), 'head', scatt...]
    ppermute x0 -> x15, starting transfers between devices: none -> 31.3 us  [the longest x7 31.2 us: ring_gather(): later.append(lax.ppermute(later[-1], axis, down))]
    ppermute x0 -> x15, waiting for transfers between devices: none -> 30.6 us  [the longest x8 30.5 us: ring_gather(): earlier.append(lax.ppermute(earlier[-1], axis, up))]
    all_gather x1, waiting for transfers between devices: 7.44 us -> 36.7 us  [body(): lax.all_gather(f_value, 'dp', axis=0, tiled=True)]
  transfers between devices with their start and end apart: 13 -> 27, of which waited for: 11 -> 18; matrix products, arithmetic and copies ran while one was open for 11% -> 12% of each run, Pallas kernels for 0% -> 0%
where the time goes in v1:
time: 797 us; the launch traced here: 789 us
  waiting for transfers between devices  469 us (59%)
  matrix products  147 us (18%)
  local copies, waits for them, and re-layouts  71.2 us (9%)
  other arithmetic  42.1 us (5%)
  starting transfers between devices  33 us (4%)
  between operations  15.7 us (2%)
  blocking collectives  10.1 us (1%)
    reduce_scatter x1, waiting for transfers between devices, body(): lax.psum_scatter(jnp.concatenate([matmul_left_t(mid_all, joined), matmul_...  107 us
    psum x1, waiting for transfers between devices, body(): lax.psum(matmul_left_t(gathered, d_query_pre).astype(jnp.bfloat16), 'dp')  93 us
    dot_general x8, matrix products, matmul(): return jnp.dot(left_side, right_side, preferred_element_type=jnp.float32)  39.1 us
    unnamed x141, local copies, waits for them, and re-layouts  36.9 us
    all_gather x1, waiting for transfers between devices, body(): lax.all_gather(f_value, 'dp', axis=0, tiled=True)  36.7 us
    dot_general x8, matrix products, matmul_right_t(): lax.dot_general(left_side, right_side, (((1,), (1,)), ((), ())), preferre...  35.5 us
    all_gather x1, waiting for transfers between devices, body(): lax.all_gather(normed.astype(jnp.bfloat16), 'head', axis=0, tiled=True)  33.8 us
    all_gather x1, waiting for transfers between devices, body(): lax.all_gather(mid_normed.astype(jnp.bfloat16), 'head', axis=0, tiled=True)  33.5 us
  transfers between devices with their start and end apart: 27, of which 18 were waited for; matrix products, arithmetic and copies ran while one was open for 12% of the time, Pallas kernels for 0%

profile of v1, /device:TPU:0, one launch (start us, length us, event | category | flops | bytes accessed | tf_op | source)
XLA Modules:
  0.0 788.7 jit_solution(3718567665374630111)
XLA Ops:
  14.2 33.8 %all-gather.7.cloned.1.call-done = bf16[1024,1024]{1,0:T(8,128)(2,1)} async-done(((bf16[512,1024]{1,0:T(8,128)(2,1)}), bf16[1024,1024]{1,0:T(8,128)(2,1)}) %all-gather.7.cloned.1.call-update) | async-done | bytes 2097168 | tf_op jit(solution)/shard_map/all_gather | solution.py:176
  47.9 4.4 multiply_convert_fusion.8
  61.0 3.1 multiply_convert_fusion.7
  68.3 15.1 %while.40 = (s32[]{:T(128)}, f32[1,4,128,128]{3,2,1,0:T(8,128)S(1)}, f32[2,1,4,512,128]{4,3,2,1,0:T(8,128)}, f32[2,1,4,128,128]{4,3,2,1,0:T(8,128)}, f32[4]{0:T(...) while((s32[]{:T(128)}, ...), condition=%wide.region_2.3_spmd.clone.clone.clone, body=%wide.region_1.2_spmd.clone.clone.clone.sunk | while | flops 1347751936 | bytes 17343232 | solution.py:107
  85.5 4.1 copy.42
  91.7 5.2 psum.49
  97.0 4.5 multiply_convert_fusion.6
  108.3 7.6 collective-permute-done
  115.9 4.4 collective-permute-start.8
  120.3 3.2 collective-permute-done.1
  123.5 4.5 collective-permute-start.9
  128.1 3.2 collective-permute-done.2
  131.3 4.4 collective-permute-start.10
  135.7 3.3 collective-permute-done.3
  139.0 4.4 collective-permute-start.11
  143.4 3.3 collective-permute-done.4
  146.7 4.4 collective-permute-start.12
  151.1 3.3 collective-permute-done.5
  154.4 4.4 collective-permute-start.13
  158.9 3.4 collective-permute-done.6
  162.4 4.5 collective-permute-start.14
  166.9 3.3 collective-permute-done.7
  205.2 14.0 %all-gather.13.cloned.1.call-done = bf16[1408,1024]{0,1:T(8,128)(2,1)} async-done(((bf16[1408,64]{0,1:T(8,128)(2,1)}), bf16[1408,1024]{0,1:T(8,128)(2,1)}) %all-gather.13.cloned.1.call-update) | async-done | bytes 2883600 | tf_op jit(solution)/shard_map/all_gather | solution.py:200
  219.2 8.4 %fusion.164 = f32[1024,1408]{1,0:T(8,128)} fusion(bf16[1024,1024]{1,0:T(8,128)(2,1)} %all-gather.15.cloned.1.call-done, bf16[1408,1024]{0,1:T(8,128)(2,1)} %all-gather.13.cloned.1.call-done), kind=kOutput, calls=%fused_computation.248 | convolution fusion | flops 2952790016 | bytes 10747904 | tf_op jit(solution)/shard_map/dot_general | solution.py:47
  227.6 36.7 %all-gather.11.cloned.1.call-done = bf16[1024,1408]{1,0:T(8,128)(2,1)} async-done(((bf16[64,1408]{1,0:T(8,128)(2,1)}), bf16[1024,1408]{1,0:T(8,128)(2,1)}) %all-gather.11.cloned.1.call-update) | async-done | bytes 2883600 | tf_op jit(solution)/shard_map/all_gather | solution.py:197
  264.4 33.5 %all-gather.9.cloned.1.call-done = bf16[1024,1024]{1,0:T(8,128)(2,1)} async-done(((bf16[512,1024]{1,0:T(8,128)(2,1)}), bf16[1024,1024]{1,0:T(8,128)(2,1)}) %all-gather.9.cloned.1.call-update) | async-done | bytes 2097168 | tf_op jit(solution)/shard_map/all_gather | solution.py:195
  297.9 6.0 fusion.163
  303.9 7.8 multiply_convert_fusion
  311.8 7.3 fusion.165
  319.1 6.5 add_convert_fusion.1
  325.7 31.9 %reduce-scatter.10.cloned.1.call-done = bf16[512,1024]{1,0:T(8,128)(2,1)} async-done(((bf16[1024,1024]{1,0:T(8,128)(2,1)}), bf16[512,1024]{1,0:T(8,128)(2,1)}) %reduce-scatter.10.cloned.1.call-update) | async-done | bytes 1048592 | tf_op jit(solution)/shard_map/reduce_scatter | solution.py:213
  365.2 29.5 %all-gather.17.cloned.1.call-done = bf16[1024,1024]{1,0:T(8,128)(2,1)} async-done(((bf16[512,1024]{1,0:T(8,128)(2,1)}), bf16[1024,1024]{1,0:T(8,128)(2,1)}) %all-gather.17.cloned.1.call-update) | async-done | bytes 2097168 | tf_op jit(solution)/shard_map/all_gather | solution.py:235
  394.8 5.3 multiply_reduce_fusion
  400.1 4.9 psum.50
  412.9 36.7 %while.41 = (s32[]{:T(128)}, f32[1,4,128,128]{3,2,1,0:T(8,128)S(1)}, f32[2,1,4,512,128]{4,3,2,1,0:T(8,128)}, f32[2,1,4,512,128]{4,3,2,1,0:T(8,128)}, bf16[2,1,4,...) while((s32[]{:T(128)}, ...), condition=%wide.region_13.14_spmd.clone.clone.clone, body=%wide.region_12.13_spmd.clone.clone.clone.sunk | while | flops 2964131840 | bytes 44889964 | solution.py:146
  420.5 3.3 fusion.272
  423.9 3.3 fusion.275
  438.8 3.3 fusion.272
  442.1 3.3 fusion.275
  480.8 7.5 convolution_convert_fusion.1
  488.6 6.1 convolution_convert_fusion
  494.8 6.8 fusion.121
  501.6 3.8 pad_maximum_fusion
  505.4 93.0 %all-reduce.3.cloned.1.call-done = (bf16[1024,512]{1,0:T(8,128)(2,1)}, bf16[1024,512]{1,0:T(8,128)(2,1)}, bf16[1024,512]{1,0:T(8,128)(2,1)}, bf16[1024,512]{1,0:T(8,128)(2,1)}, bf16[512,1024]{1,0:T(8,128)(2,1)}) async-done(((bf16[1024,512]{1,0:T(8,128)(2,1)}, bf16[1024,512]{1,0:T(8,128)(2,1)}, bf16[1024,512]{1,0:T(8,128)(2,1)}, bf16[1024,512]{1,0:T(8,128)(2,1)}, bf16[512,1024]{1,0:T(8,128)(2,1)}), ...) | async-done | bytes 5242896 | tf_op jit(solution)/shard_map/psum | solution.py:259
  607.8 25.1 %reduce-scatter.12.cloned.1.call-done = bf16[512,1024]{1,0:T(8,128)(2,1)} async-done(((bf16[1024,1024]{1,0:T(8,128)(2,1)}), bf16[512,1024]{1,0:T(8,128)(2,1)}) %reduce-scatter.12.cloned.1.call-update) | async-done | bytes 1048592 | tf_op jit(solution)/shard_map/reduce_scatter | solution.py:249
  634.7 32.4 %reduce-scatter.8.cloned.1.call-done = bf16[512,1024]{1,0:T(8,128)(2,1)} async-done(((bf16[1024,1024]{1,0:T(8,128)(2,1)}), bf16[512,1024]{1,0:T(8,128)(2,1)}) %reduce-scatter.8.cloned.1.call-update) | async-done | bytes 1048592 | tf_op jit(solution)/shard_map/reduce_scatter | solution.py:204
  667.1 4.4 fusion.135
  671.5 107.3 %reduce-scatter.14.cloned.1.call-done = bf16[64,4224]{1,0:T(8,128)(2,1)} async-done(((bf16[1024,4224]{1,0:T(8,128)(2,1)}), bf16[64,4224]{1,0:T(8,128)(2,1)}) %reduce-scatter.14.cloned.1.call-update) | async-done | bytes 540688 | tf_op jit(solution)/shard_map/reduce_scatter | solution.py:224
  (301 shorter events, 163.7 us)
Async XLA Ops:
  7.2 95.3 %copy-start = (bf16[512,1024]{1,0:T(8,128)(2,1)S(1)}, bf16[512,1024]{1,0:T(8,128)(2,1)}, u32[]{:S(2)}) copy-start(bf16[512,1024]{1,0:T(8,128)(2,1)} %param.23) | copy-start | bytes 3145732
  7.2 40.8 %all-gather.7.cloned.1.call-start = ((), (), s32[]{:S(2)}) async-start(), calls=%async_computation.5 | async-start | bytes 3145728 | tf_op jit(solution)/shard_map/all_gather | solution.py:176
  9.4 38.5 %copy-start.58 = (bf16[1024,512]{1,0:T(8,128)(2,1)S(1)}, bf16[1024,512]{1,0:T(8,128)(2,1)}, u32[]{:S(2)}) copy-start(bf16[1024,512]{1,0:T(8,128)(2,1)} %param.20) | copy-start | bytes 3145732
  12.0 181.8 %reduce-scatter.6.cloned.1.call-start = ((), (), s32[]{:S(2)}) async-start(), calls=%async_computation.6 | async-start | bytes 3145728 | tf_op jit(solution)/shard_map/reduce_scatter | solution.py:190
  91.7 9.7 %copy-start.4 = (f32[64,8,2,512]{3,1,2,0:T(8,128)}, f32[64,8,2,512]{3,1,2,0:T(8,128)S(1)}, u32[]{:S(2)}) copy-start(f32[64,8,2,512]{3,1,2,0:T(8,128)S(1)} %copy.52) | copy-start | bytes 6291460
  105.1 100.1 %all-gather.15.cloned.1.call-start = ((), (), s32[]{:S(2)}) async-start(), calls=%async_computation.11 | async-start | bytes 3145728 | tf_op jit(solution)/shard_map/all_gather | solution.py:209
  107.6 111.7 %all-gather.13.cloned.1.call-start = ((), (), s32[]{:S(2)}) async-start(), calls=%async_computation.9 | async-start | bytes 3063808 | tf_op jit(solution)/shard_map/all_gather | solution.py:200
  108.2 156.2 %all-gather.11.cloned.1.call-start = ((), (), s32[]{:S(2)}) async-start(), calls=%async_computation.8 | async-start | bytes 3063808 | tf_op jit(solution)/shard_map/all_gather | solution.py:197
  108.2 7.7 collective-permute-start
  115.9 7.6 collective-permute-start.1
  115.9 7.6 collective-permute-start.8
  123.5 7.7 collective-permute-start.2
  123.5 7.7 collective-permute-start.9
  131.2 49.1 %copy-start.46 = (bf16[64,1408]{1,0:T(8,128)(2,1)}, bf16[64,1408]{1,0:T(8,128)(2,1)S(1)}, u32[]{:S(2)}) copy-start(bf16[64,1408]{1,0:T(8,128)(2,1)S(1)} %collective-permute-done.2) | copy-start | bytes 540676
  131.2 7.7 collective-permute-start.3
  131.3 7.7 collective-permute-start.10
  139.0 41.3 %copy-start.49 = (bf16[64,1408]{1,0:T(8,128)(2,1)}, bf16[64,1408]{1,0:T(8,128)(2,1)S(1)}, u32[]{:S(2)}) copy-start(bf16[64,1408]{1,0:T(8,128)(2,1)S(1)} %collective-permute-done.3) | copy-start | bytes 540676
  139.0 7.7 collective-permute-start.4
  139.0 7.7 collective-permute-start.11
  146.7 33.6 %copy-start.51 = (bf16[64,1408]{1,0:T(8,128)(2,1)}, bf16[64,1408]{1,0:T(8,128)(2,1)S(1)}, u32[]{:S(2)}) copy-start(bf16[64,1408]{1,0:T(8,128)(2,1)S(1)} %collective-permute-done.4) | copy-start | bytes 540676
  146.7 7.7 collective-permute-start.5
  146.7 33.6 %copy-start.45 = (bf16[64,1408]{1,0:T(8,128)(2,1)}, bf16[64,1408]{1,0:T(8,128)(2,1)S(1)}, u32[]{:S(2)}) copy-start(bf16[64,1408]{1,0:T(8,128)(2,1)S(1)} %collective-permute-done.11) | copy-start | bytes 540676
  146.7 7.7 collective-permute-start.12
  154.4 25.9 %copy-start.53 = (bf16[64,1408]{1,0:T(8,128)(2,1)}, bf16[64,1408]{1,0:T(8,128)(2,1)S(1)}, u32[]{:S(2)}) copy-start(bf16[64,1408]{1,0:T(8,128)(2,1)S(1)} %collective-permute-done.5) | copy-start | bytes 540676
  154.4 7.8 collective-permute-start.6
  154.4 26.6 %copy-start.48 = (bf16[64,1408]{1,0:T(8,128)(2,1)}, bf16[64,1408]{1,0:T(8,128)(2,1)S(1)}, u32[]{:S(2)}) copy-start(bf16[64,1408]{1,0:T(8,128)(2,1)S(1)} %collective-permute-done.12) | copy-start | bytes 540676
  154.4 7.9 %collective-permute-start.13 = (bf16[64,1408]{1,0:T(8,128)(2,1)S(1)}, bf16[64,1408]{1,0:T(8,128)(2,1)}, u32[]{:S(2)}, u32[]{:S(2)}) collective-permute-start(bf16[64,1408]{1,0:T(8,128)(2,1)S(1)} %collective-permute-done.12), channel_id=1, source_target_pairs={{0,30},{2,0},{4,2},{6,4},{8,6},{10,8},{12,10},{14,12},{16,14},{18,... | collective-permute-start | bytes 540680 | tf_op jit(solution)/shard_map/ppermute | solution.py:22
  162.3 7.9 %collective-permute-start.7 = (bf16[64,1408]{1,0:T(8,128)(2,1)}, bf16[64,1408]{1,0:T(8,128)(2,1)}, u32[]{:S(2)}, u32[]{:S(2)}) collective-permute-start(bf16[64,1408]{1,0:T(8,128)(2,1)} %collective-permute-done.6), channel_id=1, source_target_pairs={{0,2},{2,4},{4,6},{6,8},{8,10},{10,12},{12,14},{14,16},{16,18},{18... | collective-permute-start | bytes 540680 | tf_op jit(solution)/shard_map/ppermute | solution.py:20
  162.3 135.6 %all-gather.9.cloned.1.call-start = ((), (), s32[]{:S(2)}) async-start(), calls=%async_computation.7 | async-start | bytes 3145728 | tf_op jit(solution)/shard_map/all_gather | solution.py:195
  162.4 21.0 %collective-permute-start.14 = (bf16[64,1408]{1,0:T(8,128)(2,1)}, bf16[64,1408]{1,0:T(8,128)(2,1)S(1)}, u32[]{:S(2)}, u32[]{:S(2)}) collective-permute-start(bf16[64,1408]{1,0:T(8,128)(2,1)} %collective-permute-done.13), channel_id=1, source_target_pairs={{0,30},{2,0},{4,2},{6,4},{8,6},{10,8},{12,10},{14,12},{16,14},{18,... | collective-permute-start | bytes 540680 | tf_op jit(solution)/shard_map/ppermute | solution.py:22
  181.0 8.0 %copy-start.52 = (bf16[64,1408]{1,0:T(8,128)(2,1)S(1)}, bf16[64,1408]{1,0:T(8,128)(2,1)}, u32[]{:S(2)}) copy-start(bf16[64,1408]{1,0:T(8,128)(2,1)} %copy-done.51) | copy-start | bytes 540676
  181.0 8.7 %copy-start.50 = (bf16[64,1408]{1,0:T(8,128)(2,1)S(1)}, bf16[64,1408]{1,0:T(8,128)(2,1)}, u32[]{:S(2)}) copy-start(bf16[64,1408]{1,0:T(8,128)(2,1)} %copy-done.49) | copy-start | bytes 540676
  181.0 9.3 %copy-start.47 = (bf16[64,1408]{1,0:T(8,128)(2,1)S(1)}, bf16[64,1408]{1,0:T(8,128)(2,1)}, u32[]{:S(2)}) copy-start(bf16[64,1408]{1,0:T(8,128)(2,1)} %copy-done.46) | copy-start | bytes 540676
  181.7 12.1 %copy-start.2 = (bf16[512,1024]{1,0:T(8,128)(2,1)S(1)}, bf16[512,1024]{1,0:T(8,128)(2,1)}, u32[]{:S(2)}) copy-start(bf16[512,1024]{1,0:T(8,128)(2,1)} %param.16) | copy-start | bytes 3145732
  183.4 9.7 %copy-start.54 = (bf16[64,1408]{1,0:T(8,128)(2,1)}, bf16[64,1408]{1,0:T(8,128)(2,1)S(1)}, u32[]{:S(2)}) copy-start(bf16[64,1408]{1,0:T(8,128)(2,1)S(1)} %collective-permute-done.14) | copy-start | bytes 540676
  196.9 160.8 %reduce-scatter.10.cloned.1.call-start = ((), (), s32[]{:S(2)}) async-start(), calls=%async_computation.12 | async-start | bytes 3145728 | tf_op jit(solution)/shard_map/reduce_scatter | solution.py:213
  311.8 7.4 copy-start.19
  325.7 69.1 %all-gather.17.cloned.1.call-start = ((), (), s32[]{:S(2)}) async-start(), calls=%async_computation.13 | async-start | bytes 3145728 | tf_op jit(solution)/shard_map/all_gather | solution.py:235
  361.5 33.3 %copy-start.5 = (f32[64,8,2,512]{3,1,2,0:T(8,128)S(1)}, f32[64,8,2,512]{3,1,2,0:T(8,128)}, u32[]{:S(2)}) copy-start(f32[64,8,2,512]{3,1,2,0:T(8,128)} %copy-done.4) | copy-start | bytes 6291460
  361.5 237.0 %all-reduce.3.cloned.1.call-start = ((), (), s32[]{:S(2)}) async-start(), calls=%async_computation.16 | async-start | bytes 10485760 | tf_op jit(solution)/shard_map/psum | solution.py:259
  456.4 11.0 %copy-start.40 = (bf16[1,2,512,4,128]{4,3,2,1,0:T(4,128)(2,1)}, bf16[1,2,512,4,128]{4,3,2,1,0:T(4,128)(2,1)S(1)}, u32[]{:S(2)}) copy-start(bf16[1,2,512,4,128]{4,3,2,1,0:T(4,128)(2,1)S(1)} %copy.46) | copy-start | bytes 3145732
  472.0 160.9 %reduce-scatter.12.cloned.1.call-start = ((), (), s32[]{:S(2)}) async-start(), calls=%async_computation.14 | async-start | bytes 3145728 | tf_op jit(solution)/shard_map/reduce_scatter | solution.py:249
  480.8 186.3 %reduce-scatter.8.cloned.1.call-start = ((), (), s32[]{:S(2)}) async-start(), calls=%async_computation.10 | async-start | bytes 3145728 | tf_op jit(solution)/shard_map/reduce_scatter | solution.py:204
  488.4 290.4 %reduce-scatter.14.cloned.1.call-start = ((), (), s32[]{:S(2)}) async-start(), calls=%async_computation.15 | async-start | bytes 9191424 | tf_op jit(solution)/shard_map/reduce_scatter | solution.py:224
  606.2 26.7 %copy-start.3 = (bf16[512,1024]{1,0:T(8,128)(2,1)S(1)}, bf16[512,1024]{1,0:T(8,128)(2,1)}, u32[]{:S(2)}) copy-start(bf16[512,1024]{1,0:T(8,128)(2,1)} %param.16) | copy-start | bytes 3145732
  606.2 26.7 %copy-start.56 = (f32[512]{0:T(512)S(1)}, f32[512]{0:T(512)}, u32[]{:S(2)}) copy-start(f32[512]{0:T(512)} %copy-done.55) | copy-start | bytes 6148
  606.2 60.8 %copy-start.12 = (bf16[512,1024]{1,0:T(8,128)(2,1)S(1)}, bf16[512,1024]{1,0:T(8,128)(2,1)}, u32[]{:S(2)}) copy-start(bf16[512,1024]{1,0:T(8,128)(2,1)} %reduce-scatter.6.cloned.1.call-done) | copy-start | bytes 3145732
  667.1 114.6 %copy-start.1 = (bf16[512,1024]{1,0:T(8,128)(2,1)S(1)}, bf16[512,1024]{1,0:T(8,128)(2,1)}, u32[]{:S(2)}) copy-start(bf16[512,1024]{1,0:T(8,128)(2,1)} %param.23) | copy-start | bytes 3145732
  (49 other events, 136.4 us)
Sparse Core Ops, SparseCore 0:
  12.1 35.8 all-gather.6
  105.3 31.8 reduce-scatter.5
  139.3 33.0 all-gather.14
  174.8 44.3 all-gather.12
  221.6 42.6 all-gather.10
  266.4 31.4 all-gather.8
  325.8 31.8 reduce-scatter.9
  361.6 33.1 all-gather.16
  472.1 126.2 all-reduce.2
  601.2 31.6 reduce-scatter.11
  635.2 31.8 reduce-scatter.7
  671.5 107.2 reduce-scatter.13
